TPU v7x, 32 devices: a whole 2x2x4 slice. The times are simulated.
32 devices in a mesh: shard: 2 (over x), ctx: 4 (over z), tp: 4 (over y, core).
Axes of the slice: x: 2, y: 2, z: 4, core: 2. Of those that a mesh axis runs over, the one named last changes fastest.
Arguments:
- tokens: bfloat16 [6, 1024, 1152], P('shard', 'ctx'), may hold values from -6 to 6
- condition: bfloat16 [6, 1152], P('shard'), may hold values from -6 to 6
- ada_weight: bfloat16 [1152, 6912], P('shard'), may hold values from -0.1875 to 0.1875
- ada_bias: float32 [6912], replicated, may hold values from -3 to 3
- qkv_weight: bfloat16 [1152, 16, 216], P('shard', 'tp'), may hold values from -0.1875 to 0.1875
- qv_bias: float32 [16, 144], P('tp'), may hold values from -2 to 2
- out_weight: bfloat16 [1152, 1152], P('tp', 'shard'), may hold values from -1 to 1
- out_bias: float32 [1152], replicated, may hold values from -2 to 2
- up_weight: bfloat16 [1152, 4608], P('shard', 'tp'), may hold values from -0.1875 to 0.1875
- up_bias: float32 [4608], P('tp'), may hold values from -3 to 3
- down_weight: bfloat16 [4608, 1152], P('tp', 'shard'), may hold values from -0.09375 to 0.09375
- down_bias: float32 [1152], replicated, may hold values from -2 to 2
- cotangent: bfloat16 [6, 1024, 1152], P('shard', 'ctx'), may hold values from -6 to 6
Outputs:
- result: bfloat16 [6, 1024, 1152], P('shard', 'ctx')
- grad_tokens: float32 [6, 1024, 1152], P('shard', 'ctx')
- grad_condition: float32 [6, 1152], P('shard')
- grad_ada_weight: float32 [1152, 6912], P('shard')
- grad_ada_bias: float32 [6912], P('shard')
- grad_qkv_weight: float32 [1152, 16, 216], P('shard', 'tp')
- grad_qv_bias: float32 [16, 144], P('tp', 'shard')
- grad_out_weight: float32 [1152, 1152], P('tp', 'shard')
- grad_out_bias: float32 [1152], P('shard')
- grad_up_weight: float32 [1152, 4608], P('shard', 'tp')
- grad_up_bias: float32 [4608], P(('tp', 'shard'))
- grad_down_weight: float32 [4608, 1152], P('tp', 'shard')
- grad_down_bias: float32 [1152], P('shard')
All inputs are finite; a program needn't handle non-finite values.
Results may differ from a plain program's by a relative error of at most 0.02.
The roundings to bfloat16 on the way count: a program that leaves them out, or rounds other values in their place, can miss the bound.
Values may be sent and summed in bfloat16 or wider, within the bound.
A program may use at most 192 MiB of HBM per device.

v0:
```python
import jax
import jax.numpy as jnp
from jax import lax
from jax.sharding import PartitionSpec as P


def layer_norm(values):
    row_mean = jnp.mean(values, -1, keepdims=True)
    centered = values - row_mean
    variance = jnp.mean(centered * centered, -1, keepdims=True)
    return centered * lax.rsqrt(variance + 1e-06)


def modulate(values, shift_row, scale_row):
    return layer_norm(values) * (1.0 + scale_row[:, None, :]) + shift_row[:, None, :]


def gelu_tanh(values):
    return (
        0.5
        * values
        * (1.0 + jnp.tanh(0.7978845608028654 * (values + 0.044715 * values * values * values)))
    )


def silu_act(values):
    return values * jax.nn.sigmoid(values)


def contract_rows(left, right):
    return lax.dot_general(
        left, right, (((0,), (0,)), ((), ())), preferred_element_type=jnp.float32
    )


def contract_cols(left, right):
    return lax.dot_general(
        left, right, (((1,), (1,)), ((), ())), preferred_element_type=jnp.float32
    )


def attend_forward(packed):
    head_size = packed.shape[-1] // 3

    def one_latent(latent_qkv):
        query_part = latent_qkv[..., :head_size]
        key_part = latent_qkv[..., head_size : 2 * head_size]
        value_part = latent_qkv[..., 2 * head_size :]
        scores = jnp.einsum(
            "shd,thd->hst", query_part, key_part, preferred_element_type=jnp.float32
        ) * head_size ** (-0.5)
        row_max = jnp.max(scores, -1, keepdims=True)
        exponent = jnp.exp(scores - row_max)
        exp_total = jnp.sum(exponent, -1, keepdims=True)
        probability = (exponent / exp_total).astype(jnp.bfloat16)
        attended = jnp.einsum(
            "hst,thd->shd", probability, value_part, preferred_element_type=jnp.float32
        )
        log_total = (row_max + jnp.log(exp_total))[..., 0]
        return (attended.astype(jnp.bfloat16), log_total)

    attended, log_total = lax.map(one_latent, packed)
    return (attended, log_total, packed)


def attend_backward(inputs):
    latent_qkv, log_total, grad_out = inputs
    head_size = latent_qkv.shape[-1] // 3
    scale_factor = head_size ** (-0.5)
    query_part = latent_qkv[..., :head_size]
    key_part = latent_qkv[..., head_size : 2 * head_size]
    value_part = latent_qkv[..., 2 * head_size :]
    scores = (
        jnp.einsum("shd,thd->hst", query_part, key_part, preferred_element_type=jnp.float32)
        * scale_factor
    )
    probability = jnp.exp(scores - log_total[..., None])
    prob_low = probability.astype(jnp.bfloat16)
    grad_prob = jnp.einsum("shd,thd->hst", grad_out, value_part, preferred_element_type=jnp.float32)
    row_dot = jnp.sum(probability * grad_prob, -1, keepdims=True)
    grad_scores = (probability * (grad_prob - row_dot)).astype(jnp.bfloat16)
    grad_query = (
        jnp.einsum("hst,thd->shd", grad_scores, key_part, preferred_element_type=jnp.float32)
        * scale_factor
    )
    grad_key = (
        jnp.einsum("hst,shd->thd", grad_scores, query_part, preferred_element_type=jnp.float32)
        * scale_factor
    )
    grad_value = jnp.einsum("hst,shd->thd", prob_low, grad_out, preferred_element_type=jnp.float32)
    return jnp.concatenate([grad_query, grad_key, grad_value], -1).astype(jnp.bfloat16)


def swap(values, axis, distance):
    count = lax.axis_size(axis)
    return lax.ppermute(values, axis, [(i, i ^ distance) for i in range(count)])


def gather_shard(values, axis):
    if lax.axis_size("shard") != 2:
        return lax.all_gather(values, "shard", axis=axis, tiled=True)
    other = swap(values, "shard", 1)
    first = lax.axis_index("shard") == 0
    return jnp.concatenate([jnp.where(first, values, other), jnp.where(first, other, values)], axis)


def scatter_shard(values, axis):
    count = lax.axis_size("shard")
    if count != 2:
        return lax.psum_scatter(
            values.astype(jnp.bfloat16), "shard", scatter_dimension=axis, tiled=True
        ).astype(jnp.float32)
    half = values.shape[axis] // 2
    low = lax.slice_in_dim(values, 0, half, axis=axis)
    high = lax.slice_in_dim(values, half, 2 * half, axis=axis)
    first = lax.axis_index("shard") == 0
    sent = jnp.where(first, high, low).astype(jnp.bfloat16)
    kept = jnp.where(first, low, high)
    return kept + swap(sent, "shard", 1).astype(jnp.float32)


def sum_axis(values, axis):
    count = lax.axis_size(axis)
    if count & count - 1:
        return lax.psum(values, axis)
    distance = 1
    while distance < count:
        values = values + swap(values, axis, distance)
        distance *= 2
    return values


def local(
    tokens,
    condition,
    ada_weight,
    ada_bias,
    qkv_weight,
    qv_bias,
    out_weight,
    out_bias,
    up_weight,
    up_bias,
    down_weight,
    down_bias,
    cotangent,
):
    lat_count, local_len, model_width = tokens.shape
    head_local = qkv_weight.shape[1]
    head_size = qv_bias.shape[1] // 2
    row_count = lat_count * local_len
    shard_count = lax.axis_size("shard")
    shard_at = lax.axis_index("shard")
    stored = ada_weight.shape[0]
    cond_float = condition.astype(jnp.float32)
    cond_act = silu_act(cond_float).astype(jnp.bfloat16)
    cond_all = (
        lax.all_gather(cond_act, "shard", axis=0, tiled=True)
        if shard_count != 2
        else gather_shard(cond_act, 0)
    )
    cond_mine = lax.dynamic_slice_in_dim(cond_all, shard_at * stored, stored, 1)
    mod_part = jnp.dot(cond_mine, ada_weight, preferred_element_type=jnp.float32)
    if shard_count == 2:
        first = shard_at == 0
        mod_low, mod_high = (mod_part[:lat_count], mod_part[lat_count:])
        mod_raw = jnp.where(first, mod_low, mod_high) + swap(
            jnp.where(first, mod_high, mod_low), "shard", 1
        )
    else:
        mod_raw = lax.psum_scatter(mod_part, "shard", scatter_dimension=0, tiled=True)
    qkv_full = gather_shard(qkv_weight.reshape(stored, -1), 0)
    out_full = gather_shard(out_weight, 1)
    up_full = gather_shard(up_weight, 0)
    down_full = gather_shard(down_weight, 1)
    modulation = (mod_raw + ada_bias).reshape(lat_count, 6, model_width)
    tok_float = tokens.astype(jnp.float32)
    normed = (
        modulate(tok_float, modulation[:, 0], modulation[:, 1])
        .astype(jnp.bfloat16)
        .reshape(row_count, model_width)
    )
    qkv_bias = jnp.concatenate(
        [
            qv_bias[:, :head_size],
            jnp.zeros((head_local, head_size), jnp.float32),
            qv_bias[:, head_size:],
        ],
        1,
    )
    qkv_flat = qkv_full
    packed = jnp.dot(normed, qkv_flat, preferred_element_type=jnp.float32).reshape(
        lat_count, local_len, head_local, 3 * head_size
    )
    packed = (packed + qkv_bias).astype(jnp.bfloat16)
    attended, log_total, head_packed = attend_forward(
        lax.all_to_all(packed, "ctx", split_axis=2, concat_axis=1, tiled=True)
    )
    attn_rows = lax.all_to_all(attended, "ctx", split_axis=1, concat_axis=2, tiled=True).reshape(
        row_count, head_local * head_size
    )
    branch = (
        lax.psum(
            jnp.dot(attn_rows, out_full, preferred_element_type=jnp.float32).astype(jnp.bfloat16),
            "tp",
        ).astype(jnp.float32)
        + out_bias
    )
    branch = branch.reshape(lat_count, local_len, model_width)
    middle = tok_float + modulation[:, 2][:, None, :] * branch
    normed_two = (
        modulate(middle, modulation[:, 3], modulation[:, 4])
        .astype(jnp.bfloat16)
        .reshape(row_count, model_width)
    )
    up_proj = jnp.dot(normed_two, up_full, preferred_element_type=jnp.float32) + up_bias
    activated = gelu_tanh(up_proj).astype(jnp.bfloat16)
    down_proj = (
        lax.psum(
            jnp.dot(activated, down_full, preferred_element_type=jnp.float32).astype(jnp.bfloat16),
            "tp",
        ).astype(jnp.float32)
        + down_bias
    )
    down_proj = down_proj.reshape(lat_count, local_len, model_width)
    result = (middle + modulation[:, 5][:, None, :] * down_proj).astype(jnp.bfloat16)
    grad_out = cotangent.astype(jnp.float32)
    grad_gate2 = jnp.sum(grad_out * down_proj, 1)
    grad_down = grad_out * modulation[:, 5][:, None, :]
    grad_down_bias = jnp.sum(grad_down, (0, 1))
    grad_down_low = grad_down.astype(jnp.bfloat16).reshape(row_count, model_width)
    grad_act = contract_cols(grad_down_low, down_full)
    grad_down_weight = contract_rows(activated, grad_down_low)
    grad_up = jax.vjp(gelu_tanh, up_proj)[1](grad_act)[0]
    grad_up_bias = jnp.sum(grad_up, 0)
    grad_up_low = grad_up.astype(jnp.bfloat16)
    grad_up_weight = contract_rows(normed_two, grad_up_low)
    grad_normed_two = (
        lax.psum(contract_cols(grad_up_low, up_full).astype(jnp.bfloat16), "tp")
        .astype(jnp.float32)
        .reshape(lat_count, local_len, model_width)
    )
    pull_two = jax.vjp(modulate, middle, modulation[:, 3], modulation[:, 4])[1]
    grad_middle_norm, grad_shift2, grad_scale2 = pull_two(grad_normed_two)
    grad_middle = grad_out + grad_middle_norm
    grad_gate1 = jnp.sum(grad_middle * branch, 1)
    grad_branch = grad_middle * modulation[:, 2][:, None, :]
    grad_out_bias = jnp.sum(grad_branch, (0, 1))
    grad_branch_low = grad_branch.astype(jnp.bfloat16).reshape(row_count, model_width)
    grad_out_weight = contract_rows(attn_rows, grad_branch_low)
    grad_attended = (
        contract_cols(grad_branch_low, out_full)
        .astype(jnp.bfloat16)
        .reshape(lat_count, local_len, head_local, head_size)
    )
    grad_heads = lax.all_to_all(grad_attended, "ctx", split_axis=2, concat_axis=1, tiled=True)
    grad_packed_heads = lax.map(attend_backward, (head_packed, log_total, grad_heads))
    grad_packed = lax.all_to_all(grad_packed_heads, "ctx", split_axis=1, concat_axis=2, tiled=True)
    bias_sums = jnp.sum(grad_packed.astype(jnp.float32), (0, 1))
    grad_qv_bias = jnp.concatenate([bias_sums[:, :head_size], bias_sums[:, 2 * head_size :]], 1)
    grad_packed_rows = grad_packed.reshape(row_count, head_local * 3 * head_size)
    grad_qkv_weight = contract_rows(normed, grad_packed_rows)
    grad_normed = (
        lax.psum(contract_cols(grad_packed_rows, qkv_flat).astype(jnp.bfloat16), "tp")
        .astype(jnp.float32)
        .reshape(lat_count, local_len, model_width)
    )
    pull_one = jax.vjp(modulate, tok_float, modulation[:, 0], modulation[:, 1])[1]
    grad_tokens_norm, grad_shift1, grad_scale1 = pull_one(grad_normed)
    grad_tokens = grad_middle + grad_tokens_norm
    grad_mod_part = jnp.stack(
        [grad_shift1, grad_scale1, grad_gate1, grad_shift2, grad_scale2, grad_gate2], 1
    )
    small = jnp.concatenate(
        [
            grad_mod_part.reshape(-1),
            grad_qv_bias.reshape(-1),
            grad_out_bias,
            grad_up_bias,
            grad_down_bias,
        ]
    )
    small = sum_axis(small, "ctx")
    mod_count = lat_count * 6 * model_width
    grad_modulation = small[:mod_count].reshape(lat_count, 6 * model_width)
    bias_part = small[mod_count:]
    if shard_count == 2:
        other = swap(small, "shard", 1)
        other_mod = other[:mod_count].reshape(lat_count, 6 * model_width)
        grad_mod_all = jnp.concatenate(
            [
                jnp.where(first, grad_modulation, other_mod),
                jnp.where(first, other_mod, grad_modulation),
            ],
            0,
        )
        bias_all = bias_part + other[mod_count:]
    else:
        grad_mod_all = lax.all_gather(grad_modulation, "shard", axis=0, tiled=True)
        bias_all = lax.psum(bias_part, "shard")
    grad_ada_bias_all = jnp.sum(grad_mod_all, 0)
    grad_ada_bias = lax.dynamic_slice_in_dim(
        grad_ada_bias_all,
        shard_at * (6 * model_width // shard_count),
        6 * model_width // shard_count,
        0,
    )
    grad_mod_low = grad_mod_all.astype(jnp.bfloat16)
    grad_ada_weight = contract_rows(cond_mine, grad_mod_low)
    grad_cond_part = contract_cols(grad_mod_low, ada_weight)
    if shard_count == 2:
        part_low, part_high = (grad_cond_part[:lat_count], grad_cond_part[lat_count:])
        kept = jnp.where(first, part_low, part_high)
        got = swap(jnp.where(first, part_high, part_low), "shard", 1)
        grad_cond_act = jnp.concatenate(
            [jnp.where(first, kept, got), jnp.where(first, got, kept)], 1
        )
    else:
        grad_cond_act = lax.all_to_all(
            grad_cond_part, "shard", split_axis=0, concat_axis=1, tiled=True
        )
    grad_condition = jax.vjp(silu_act, cond_float)[1](grad_cond_act)[0]

    def pick(values, start, size, axis):
        part = size // shard_count
        return lax.dynamic_slice_in_dim(values, start + shard_at * part, part, axis)

    bias_width = head_local * 2 * head_size
    hidden = grad_up_bias.shape[0]
    qv_sum = bias_all[:bias_width].reshape(head_local, 2 * head_size)
    summed = (
        lax.psum(scatter_shard(grad_qkv_weight, 0).astype(jnp.bfloat16), "ctx")
        .astype(jnp.float32)
        .reshape(stored, head_local, 3 * head_size),
        pick(qv_sum, 0, 2 * head_size, 1),
        lax.psum(scatter_shard(grad_out_weight, 1).astype(jnp.bfloat16), "ctx").astype(jnp.float32),
        pick(bias_all, bias_width, model_width, 0),
        lax.psum(scatter_shard(grad_up_weight, 0).astype(jnp.bfloat16), "ctx").astype(jnp.float32),
        pick(bias_all, bias_width + model_width, hidden, 0),
        lax.psum(scatter_shard(grad_down_weight, 1).astype(jnp.bfloat16), "ctx").astype(
            jnp.float32
        ),
        pick(bias_all, bias_width + model_width + hidden, model_width, 0),
    )
    return (
        result,
        grad_tokens,
        grad_condition,
        grad_ada_weight,
        grad_ada_bias,
        summed[0],
        summed[1],
        summed[2],
        summed[3],
        summed[4],
        summed[5],
        summed[6],
        summed[7],
    )


def solution(mesh):
    return jax.shard_map(
        local,
        mesh=mesh,
        in_specs=(
            P("shard", "ctx", None),
            P("shard", None),
            P("shard", None),
            P(),
            P("shard", "tp", None),
            P("tp", None),
            P("tp", "shard"),
            P(),
            P("shard", "tp"),
            P("tp"),
            P("tp", "shard"),
            P(),
            P("shard", "ctx", None),
        ),
        out_specs=(
            P("shard", "ctx", None),
            P("shard", "ctx", None),
            P("shard", None),
            P("shard", None),
            P("shard"),
            P("shard", "tp", None),
            P("tp", "shard"),
            P("tp", "shard"),
            P("shard"),
            P("shard", "tp"),
            P(("tp", "shard")),
            P("tp", "shard"),
            P("shard"),
        ),
        check_vma=False,
    )
```

profile of v0, /device:TPU:0, one launch (start us, length us, event | category | flops | bytes accessed | tf_op | source)
XLA Modules:
  0.0 635.3 jit_solution(15593193496477154573)
XLA Ops:
  8.1 3.0 collective-permute-start
  16.5 4.4 fusion.83
  23.2 16.3 %collective-permute-done.1 = f32[3,6912]{1,0:T(4,128)S(1)} collective-permute-done((f32[3,6912]{1,0:T(4,128)S(1)}, f32[3,6912]{1,0:T(4,128)S(1)}, u32[]{:S(2)}, u32[]{:S(2)}) %collective-permute-start.1) | collective-permute-done | bytes 82976 | tf_op jit(solution)/shard_map/ppermute | solution.py:96
  40.9 2.5 fusion.40
  48.7 4.0 add_convert_fusion.4
  53.8 4.9 all-to-all-start
  63.5 25.8 %all-to-all-done = bf16[3,256,4,216]{1,3,0,2:T(8,128)(2,1)S(1)} async-done(((bf16[3,256,4,216]{1,3,0,2:T(8,128)(2,1)}), bf16[3,256,4,216]{1,3,0,2:T(8,128)(2,1)S(1)}, u32[]{:S(2)}, u32[]{:S(2)}) %all-to-all-start) | async-done | bytes 1327136 | tf_op jit(solution)/shard_map/all_to_all | solution.py:197
  89.5 9.3 %while.22 = (s32[]{:T(128)}, bf16[3,1024,1,72]{1,3,2,0:T(8,128)(2,1)S(1)}, f32[3,1,1024]{2,1,0:T(1,128)}, bf16[3,1024,1,216]{1,3,2,0:T(8,128)(2,1)S(1)}, s32[]{:T(128)}) while((s32[]{:T(128)}, bf16[3,1024,1,72]{1,3,2,0:T(8,128)(2,1)S(1)}, f32[3,1,1024]{2,1,0:T(1,128)}, bf16[3,1024,1,216]{1,3,2,0:T(8,128)(2,1)S(1)}, s32[]{:T(128)}) %tuple.107), condition=%wide.region_5.6_spmd, body=%wide.region_2.5_spmd.sunk | while | flops 311499776 | bytes 14098513 | solution.py:62
  101.7 3.5 all-to-all-start.1
  107.9 9.5 %all-to-all-done.1 = bf16[4,2,27648]{2,1,0:T(2,128)(2,1)S(1)} async-done(((bf16[4,2,27648]{2,1,0:T(2,128)(2,1)}), bf16[4,2,27648]{2,1,0:T(2,128)(2,1)S(1)}, u32[]{:S(2)}, u32[]{:S(2)}) %all-to-all-start.1) | async-done | bytes 442400 | tf_op jit(solution)/shard_map/all_to_all | solution.py:199
  123.6 3.1 broadcast_select_fusion.3
  126.7 3.2 broadcast_select_fusion.1
  129.9 38.0 %all-reduce.7.cloned.1.call-done = bf16[768,1152]{1,0:T(8,128)(2,1)} async-done(((bf16[768,1152]{1,0:T(8,128)(2,1)}), bf16[768,1152]{1,0:T(8,128)(2,1)}) %all-reduce.7.cloned.1.call-update) | async-done | bytes 1769488 | tf_op jit(solution)/shard_map/psum | solution.py:203
  173.8 2.7 convolution_add_fusion
  176.5 5.0 fusion.86
  181.5 6.9 %fusion.94 = (f32[1152]{0:T(1024)}, bf16[768,1152]{1,0:T(8,128)(2,1)S(1)}) fusion(f32[768,1152]{1,0:T(8,128)S(1)} %convolution_add_fusion, bf16[768,1152]{1,0:T(8,128)(2,1)S(1)} %bitcast.203, bf16[1152,576]{0,1:T(8,128)(2,1)S(1)} %copy-done.29, bf16[1152,576]{0,1:T(8,128)(2,1)S(1)} %copy-done.28), kind=kOutput, calls=%fused_computation.200 | convolution fusion | flops 2065857408 | bytes 9736704 | tf_op jit(solution)/shard_map/dot_general | solution.py:37
  188.4 3.8 convolution_convert_fusion.1
  192.3 4.0 select_convert_fusion
  197.8 4.9 fusion.60
  202.6 35.9 %all-reduce.9.cloned.1.call-done = bf16[3,256,1152]{2,1,0:T(8,128)(2,1)} async-done(((bf16[3,256,1152]{2,1,0:T(8,128)(2,1)}), bf16[3,256,1152]{2,1,0:T(8,128)(2,1)}) %all-reduce.9.cloned.1.call-update) | async-done | bytes 1769488 | tf_op jit(solution)/shard_map/psum | solution.py:239
  243.3 2.9 multiply_reduce_fusion.4
  255.3 4.8 all-to-all-start.2
  260.1 7.2 %convolution_convert_fusion.2 = bf16[768,1152]{1,0:T(8,128)(2,1)} fusion(bf16[1152,576]{0,1:T(8,128)(2,1)} %get-tuple-element.192, bf16[1152,576]{0,1:T(8,128)(2,1)} %get-tuple-element.191, f32[768,1152]{1,0:T(8,128)} %copy-done.70), kind=kOutput, calls=%fused_computation.96 | convolution fusion | flops 2052587520 | bytes 7962624 | tf_op jit(solution)/shard_map/dot_general | solution.py:220
  267.3 5.6 all-to-all-done.2
  274.6 23.0 %while.23 = (s32[]{:T(128)}, bf16[3,1024,1,216]{1,3,2,0:T(8,128)(2,1)}, bf16[3,1024,1,216]{1,3,2,0:T(8,128)(2,1)}, f32[3,1,1024]{2,1,0:T(1,128)}, bf16[3,1024,1,72]{1,3,2,0:T(8,128)(2,1)}, /*index=5*/s32[]{:T(128)}) while((s32[]{:T(128)}, bf16[3,1024,1,216]{1,3,2,0:T(8,128)(2,1)}, bf16[3,1024,1,216]{1,3,2,0:T(8,128)(2,1)}, ...), condition=%wide.region_15.16_spmd, body=%wide.region_13.15_spmd.sunk | while | flops 769252352 | bytes 36499580 | solution.py:257
  297.7 4.1 copy.179
  301.8 4.5 all-to-all-start.3
  310.4 3.9 select_convert_fusion.1
  316.6 3.8 collective-permute-done.11
  321.4 4.4 add_convert_fusion.2
  325.8 28.2 %all-to-all-done.3 = bf16[3,1024,1,216]{3,0,2,1:T(4,128)(2,1)} async-done(((bf16[3,1024,1,216]{3,0,2,1:T(4,128)(2,1)}), bf16[3,1024,1,216]{3,0,2,1:T(4,128)(2,1)}, u32[]{:S(2)}, u32[]{:S(2)}) %all-to-all-start.3) | async-done | bytes 1327136 | tf_op jit(solution)/shard_map/all_to_all | solution.py:258
  354.0 4.5 copy.190
  358.5 4.1 copy.181
  362.6 4.2 reshape.364
  366.8 5.3 convolution_convert_fusion
  372.2 4.5 add_convert_fusion.3
  380.4 4.0 fusion.95
  389.0 56.7 %all-reduce.11.cloned.1.call-done = (bf16[768,1152]{1,0:T(8,128)(2,1)}, bf16[3,256,1152]{2,1,0:T(8,128)(2,1)}) async-done(((bf16[768,1152]{1,0:T(8,128)(2,1)}, bf16[3,256,1152]{2,1,0:T(8,128)(2,1)}), (bf16[768,1152]{1,0:T(8,128)(2,1)}, bf16[3,256,1152]{2,1,0:T(8,128)(2,1)})) %all-reduce.11.cloned.1.call-update) | async-done | bytes 3538960 | tf_op jit(solution)/shard_map/psum | solution.py:219
  445.7 3.0 fusion.46
  448.8 2.7 fusion.51
  453.0 2.8 fusion.33
  459.7 3.7 add_convert_fusion.5
  470.0 8.2 %collective-permute-done.7 = f32[24768]{0:T(1024)S(1)} collective-permute-done((f32[24768]{0:T(1024)S(1)}, f32[24768]{0:T(1024)S(1)}, u32[]{:S(2)}, u32[]{:S(2)}) %collective-permute-start.7) | collective-permute-done | bytes 99104 | tf_op jit(solution)/shard_map/ppermute | solution.py:96
  479.8 4.1 add_add_fusion.2
  486.5 5.5 fusion.64
  493.3 8.2 %fusion.63 = f32[576,6912]{1,0:T(8,128)} fusion(bf16[3,6912]{1,0:T(4,128)(2,1)S(1)} %get-tuple-element.202, bf16[3,6912]{1,0:T(4,128)(2,1)S(1)} %get-tuple-element.200, s32[]{:T(128)S(6)} %select_n.170, bf16[3,1152]{1,0:T(4,128)(2,1)S(1)} %copy-done.51, bf16[3,1152]{1,0:T(4,128)(2,1)S(1)} %copy-done.49), kind=kOutput, calls=%fused_computation.137 | convolution fusion | flops 47955456 | bytes 16022020 | tf_op jit(solution)/shard_map/dot_general | solution.py:31
  502.9 117.2 %all-reduce.13.cloned.1.call-done = (bf16[576,4,216]{0,2,1:T(8,128)(2,1)}, bf16[288,576]{1,0:T(8,128)(2,1)}, bf16[576,1152]{1,0:T(8,128)(2,1)}, bf16[1152,576]{0,1:T(8,128)(2,1)}) async-done(((bf16[576,4,216]{0,2,1:T(8,128)(2,1)}, bf16[288,576]{1,0:T(8,128)(2,1)}, bf16[576,1152]{1,0:T(8,128)(2,1)}, bf16[1152,576]{0,1:T(8,128)(2,1)}), (bf16[576,4,216]{0,2,1:T(8,128)(2,1)}, bf16[288,576]{1,0:T(8,128)(2,1)}, ...) | async-done | bytes 3981328 | tf_op jit(solution)/shard_map/psum | solution.py:332
  622.1 2.8 reshape.375
  (319 shorter events, 128.1 us)
Async XLA Ops:
  7.2 8.7 %copy-start.52 = (bf16[3,1152]{1,0:T(4,128)(2,1)S(1)}, bf16[3,1152]{1,0:T(4,128)(2,1)}, u32[]{:S(2)}) copy-start(bf16[3,1152]{1,0:T(4,128)(2,1)} %param.18) | copy-start | bytes 20740
  7.2 7.5 %copy-start = (bf16[3,256,1152]{2,1,0:T(8,128)(2,1)S(1)}, bf16[3,256,1152]{2,1,0:T(8,128)(2,1)}, u32[]{:S(2)}) copy-start(bf16[3,256,1152]{2,1,0:T(8,128)(2,1)} %param.17) | copy-start | bytes 5308420
  7.2 8.1 %copy-start.68 = (f32[4,144]{1,0:T(4,128)S(1)}, f32[4,144]{1,0:T(4,128)}, u32[]{:S(2)}) copy-start(f32[4,144]{1,0:T(4,128)} %param.22) | copy-start | bytes 6916
  8.1 7.8 %collective-permute-start = (bf16[3,1152]{1,0:T(4,128)(2,1)S(1)}, bf16[3,1152]{1,0:T(4,128)(2,1)S(1)}, u32[]{:S(2)}, u32[]{:S(2)}) collective-permute-start(bf16[3,1152]{1,0:T(4,128)(2,1)S(1)} %fusion.68), channel_id=1, source_target_pairs={{0,16},{16,0},{1,17},{17,1},{2,18},{18,2},{3,19},{19,3},{4,20},{20... | collective-permute-start | bytes 20744 | tf_op jit(solution)/shard_map/ppermute | solution.py:96
  12.8 30.6 %collective-permute-start.2 = (bf16[576,864]{1,0:T(8,128)(2,1)S(1)}, bf16[576,864]{1,0:T(8,128)(2,1)}, u32[]{:S(2)}, u32[]{:S(2)}) collective-permute-start(bf16[576,864]{1,0:T(8,128)(2,1)S(1)} %copy.166), channel_id=1, source_target_pairs={{0,16},{16,0},{1,17},{17,1},{2,18},{18,2},{3,19},{19,3},{4,20},{20... | collective-permute-start | bytes 2985992 | tf_op jit(solution)/shard_map/ppermute | solution.py:96
  14.7 26.2 %copy-start.45 = (f32[3,256]{1,0:T(4,128)}, f32[3,256]{1,0:T(4,128)S(1)}, u32[]{:S(2)}) copy-start(f32[3,256]{1,0:T(4,128)S(1)} %broadcast_multiply_fusion.1) | copy-start | bytes 9220
  15.3 25.6 %copy-start.58 = (f32[3,256]{1,0:T(4,128)}, f32[3,256]{1,0:T(4,128)S(1)}, u32[]{:S(2)}) copy-start(f32[3,256]{1,0:T(4,128)S(1)} %fusion.72) | copy-start | bytes 9220
  16.5 22.9 %copy-start.64 = (f32[6912]{0:T(1024)S(1)}, f32[6912]{0:T(1024)}, u32[]{:S(2)}) copy-start(f32[6912]{0:T(1024)} %param.20) | copy-start | bytes 82948
  21.0 18.4 %collective-permute-start.1 = (f32[3,6912]{1,0:T(4,128)S(1)}, f32[3,6912]{1,0:T(4,128)S(1)}, u32[]{:S(2)}, u32[]{:S(2)}) collective-permute-start(f32[3,6912]{1,0:T(4,128)S(1)} %slice_select_fusion), channel_id=1, source_target_pairs={{0,16},{16,0},{1,17},{17,1},{2,18},{18,2},{3,19},{19,3},{4,20},{20... | collective-permute-start | bytes 248840 | tf_op jit(solution)/shard_map/ppermute | solution.py:96
  52.7 8.6 %copy-start.11 = (bf16[3,256,1152]{2,1,0:T(8,128)(2,1)S(1)}, bf16[3,256,1152]{2,1,0:T(8,128)(2,1)}, u32[]{:S(2)}) copy-start(bf16[3,256,1152]{2,1,0:T(8,128)(2,1)} %param.29) | copy-start | bytes 5308420
  53.8 35.5 %all-to-all-start = ((bf16[3,256,4,216]{1,3,0,2:T(8,128)(2,1)}), bf16[3,256,4,216]{1,3,0,2:T(8,128)(2,1)S(1)}, u32[]{:S(2)}, u32[]{:S(2)}) async-start(bf16[3,256,4,216]{1,3,0,2:T(8,128)(2,1)} %copy.169), calls=%async_computation | async-start | bytes 2654208 | tf_op jit(solution)/shard_map/all_to_all | solution.py:197
  58.7 48.0 %collective-permute-start.3 = (bf16[288,576]{1,0:T(8,128)(2,1)}, bf16[288,576]{1,0:T(8,128)(2,1)}, u32[]{:S(2)}, u32[]{:S(2)}) collective-permute-start(bf16[288,576]{1,0:T(8,128)(2,1)} %param.23), channel_id=1, source_target_pairs={{0,16},{16,0},{1,17},{17,1},{2,18},{18,2},{3,19},{19,3},{4,20},{20... | collective-permute-start | bytes 995336 | tf_op jit(solution)/shard_map/ppermute | solution.py:96
  59.2 64.3 %collective-permute-start.4 = (bf16[576,1152]{1,0:T(8,128)(2,1)}, bf16[576,1152]{1,0:T(8,128)(2,1)}, u32[]{:S(2)}, u32[]{:S(2)}) collective-permute-start(bf16[576,1152]{1,0:T(8,128)(2,1)} %param.25), channel_id=1, source_target_pairs={{0,16},{16,0},{1,17},{17,1},{2,18},{18,2},{3,19},{19,3},{4,20},{20... | collective-permute-start | bytes 3981320 | tf_op jit(solution)/shard_map/ppermute | solution.py:96
  60.7 66.0 %collective-permute-start.5 = (bf16[1152,576]{0,1:T(8,128)(2,1)}, bf16[1152,576]{0,1:T(8,128)(2,1)}, u32[]{:S(2)}, u32[]{:S(2)}) collective-permute-start(bf16[1152,576]{0,1:T(8,128)(2,1)} %param.27), channel_id=1, source_target_pairs={{0,16},{16,0},{1,17},{17,1},{2,18},{18,2},{3,19},{19,3},{4,20},{20... | collective-permute-start | bytes 3981320 | tf_op jit(solution)/shard_map/ppermute | solution.py:96
  98.8 21.0 %copy-start.7 = (bf16[3,1024,1,216]{1,3,2,0:T(8,128)(2,1)}, bf16[3,1024,1,216]{1,3,2,0:T(8,128)(2,1)S(1)}, u32[]{:S(2)}) copy-start(bf16[3,1024,1,216]{1,3,2,0:T(8,128)(2,1)S(1)} %get-tuple-element.340) | copy-start | bytes 3981316
  98.8 6.6 %copy-start.60 = (f32[3,1,1152]{2,1,0:T(1,128)S(1)}, f32[3,1,1152]{2,1,0:T(1,128)}, u32[]{:S(2)}) copy-start(f32[3,1,1152]{2,1,0:T(1,128)} %get-tuple-element.206) | copy-start | bytes 41476
  98.8 6.7 %copy-start.61 = (f32[3,1,1152]{2,1,0:T(1,128)S(1)}, f32[3,1,1152]{2,1,0:T(1,128)}, u32[]{:S(2)}) copy-start(f32[3,1,1152]{2,1,0:T(1,128)} %get-tuple-element.207) | copy-start | bytes 41476
  101.7 15.7 %all-to-all-start.1 = ((bf16[4,2,27648]{2,1,0:T(2,128)(2,1)}), bf16[4,2,27648]{2,1,0:T(2,128)(2,1)S(1)}, u32[]{:S(2)}, u32[]{:S(2)}) async-start(bf16[4,2,27648]{2,1,0:T(2,128)(2,1)} %reshape.412), calls=%async_computation.1 | async-start | bytes 884736 | tf_op jit(solution)/shard_map/all_to_all | solution.py:199
  105.2 62.7 %all-reduce.7.cloned.1.call-start = ((), (), s32[]{:S(2)}) async-start(), calls=%async_computation.4 | async-start | bytes 3538944 | tf_op jit(solution)/shard_map/psum | solution.py:203
  107.9 15.6 %copy-start.38 = (bf16[288,576]{1,0:T(8,128)(2,1)}, bf16[288,576]{1,0:T(8,128)(2,1)S(1)}, u32[]{:S(2)}) copy-start(bf16[288,576]{1,0:T(8,128)(2,1)S(1)} %get-tuple-element.195) | copy-start | bytes 995332
  107.9 15.6 %copy-start.40 = (bf16[288,576]{1,0:T(8,128)(2,1)}, bf16[288,576]{1,0:T(8,128)(2,1)S(1)}, u32[]{:S(2)}) copy-start(bf16[288,576]{1,0:T(8,128)(2,1)S(1)} %get-tuple-element.196) | copy-start | bytes 995332
  123.5 115.0 %all-reduce.9.cloned.1.call-start = ((), (), s32[]{:S(2)}) async-start(), calls=%async_computation.5 | async-start | bytes 3538944 | tf_op jit(solution)/shard_map/psum | solution.py:239
  126.7 41.2 %copy-start.66 = (f32[1152]{0:T(1024)S(1)}, f32[1152]{0:T(1024)}, u32[]{:S(2)}) copy-start(f32[1152]{0:T(1024)} %param.24) | copy-start | bytes 13828
  196.3 125.1 %collective-permute-start.13 = (bf16[1152,576]{0,1:T(8,128)(2,1)}, bf16[1152,576]{0,1:T(8,128)(2,1)}, u32[]{:S(2)}, u32[]{:S(2)}) collective-permute-start(bf16[1152,576]{0,1:T(8,128)(2,1)} %select_convert_fusion), channel_id=1, source_target_pairs={{0,16},{16,0},{1,17},{17,1},{2,18},{18,2},{3,19},{19,3},{4,20},{20... | collective-permute-start | bytes 3981320 | tf_op jit(solution)/shard_map/ppermute | solution.py:96
  255.3 17.5 %all-to-all-start.2 = ((bf16[3,256,4,72]{1,3,0,2:T(8,128)(2,1)}), bf16[3,256,4,72]{1,3,0,2:T(8,128)(2,1)}, u32[]{:S(2)}, u32[]{:S(2)}) async-start(bf16[3,256,4,72]{1,3,0,2:T(8,128)(2,1)} %copy.175), calls=%async_computation.2 | async-start | bytes 884736 | tf_op jit(solution)/shard_map/all_to_all | solution.py:256
  301.8 52.2 %all-to-all-start.3 = ((bf16[3,1024,1,216]{3,0,2,1:T(4,128)(2,1)}), bf16[3,1024,1,216]{3,0,2,1:T(4,128)(2,1)}, u32[]{:S(2)}, u32[]{:S(2)}) async-start(bf16[3,1024,1,216]{3,0,2,1:T(4,128)(2,1)} %copy.179), calls=%async_computation.3 | async-start | bytes 4194304 | tf_op jit(solution)/shard_map/all_to_all | solution.py:258
  306.2 139.4 %all-reduce.11.cloned.1.call-start = ((), (), s32[]{:S(2)}) async-start(), calls=%async_computation.6 | async-start | bytes 7077888 | tf_op jit(solution)/shard_map/psum | solution.py:219
  308.6 6.2 copy-start.55
  308.7 6.8 %copy-start.56 = (f32[3,1152]{1,0:T(4,128)S(1)}, f32[3,1152]{1,0:T(4,128)}, u32[]{:S(2)}) copy-start(f32[3,1152]{1,0:T(4,128)} %get-tuple-element.152) | copy-start | bytes 41476
  308.7 7.4 %copy-start.54 = (f32[3,1152]{1,0:T(4,128)S(1)}, f32[3,1152]{1,0:T(4,128)}, u32[]{:S(2)}) copy-start(f32[3,1152]{1,0:T(4,128)} %get-tuple-element.155) | copy-start | bytes 41476
  308.8 11.6 %collective-permute-start.11 = (bf16[288,576]{1,0:T(8,128)(2,1)S(1)}, bf16[288,576]{1,0:T(8,128)(2,1)S(1)}, u32[]{:S(2)}, u32[]{:S(2)}) collective-permute-start(bf16[288,576]{1,0:T(8,128)(2,1)S(1)} %select_convert_fusion.3), channel_id=1, source_target_pairs={{0,16},{16,0},{1,17},{17,1},{2,18},{18,2},{3,19},{19,3},{4,20},{20... | collective-permute-start | bytes 995336 | tf_op jit(solution)/shard_map/ppermute | solution.py:96
  314.2 58.0 %collective-permute-start.12 = (bf16[576,1152]{1,0:T(8,128)(2,1)}, bf16[576,1152]{1,0:T(8,128)(2,1)}, u32[]{:S(2)}, u32[]{:S(2)}) collective-permute-start(bf16[576,1152]{1,0:T(8,128)(2,1)} %select_convert_fusion.1), channel_id=1, source_target_pairs={{0,16},{16,0},{1,17},{17,1},{2,18},{18,2},{3,19},{19,3},{4,20},{20... | collective-permute-start | bytes 3981320 | tf_op jit(solution)/shard_map/ppermute | solution.py:96
  372.2 248.0 %all-reduce.13.cloned.1.call-start = ((), (), s32[]{:S(2)}) async-start(), calls=%async_computation.7 | async-start | bytes 8257536 | tf_op jit(solution)/shard_map/psum | solution.py:332
  380.4 65.3 %copy-start.46 = (f32[3,256]{1,0:T(4,128)S(1)}, f32[3,256]{1,0:T(4,128)}, u32[]{:S(2)}) copy-start(f32[3,256]{1,0:T(4,128)} %copy-done.45) | copy-start | bytes 9220
  386.4 62.3 %copy-start.63 = (f32[3,256]{1,0:T(4,128)S(1)}, f32[3,256]{1,0:T(4,128)}, u32[]{:S(2)}) copy-start(f32[3,256]{1,0:T(4,128)} %copy-done.62) | copy-start | bytes 9220
  386.4 62.3 %copy-start.59 = (f32[3,256]{1,0:T(4,128)S(1)}, f32[3,256]{1,0:T(4,128)}, u32[]{:S(2)}) copy-start(f32[3,256]{1,0:T(4,128)} %copy-done.58) | copy-start | bytes 9220
  387.5 72.1 %collective-permute-start.10 = (bf16[576,864]{1,0:T(8,128)(2,1)}, bf16[576,864]{1,0:T(8,128)(2,1)}, u32[]{:S(2)}, u32[]{:S(2)}) collective-permute-start(bf16[576,864]{1,0:T(8,128)(2,1)} %select_convert_fusion.2), channel_id=1, source_target_pairs={{0,16},{16,0},{1,17},{17,1},{2,18},{18,2},{3,19},{19,3},{4,20},{20... | collective-permute-start | bytes 2985992 | tf_op jit(solution)/shard_map/ppermute | solution.py:96
  445.7 7.0 %copy-start.23 = (bf16[768,1152]{1,0:T(8,128)(2,1)S(1)}, bf16[768,1152]{1,0:T(8,128)(2,1)}, u32[]{:S(2)}) copy-start(bf16[768,1152]{1,0:T(8,128)(2,1)} %get-tuple-element.175) | copy-start | bytes 5308420
  445.7 7.0 %copy-start.67 = (f32[1152]{0:T(1024)S(1)}, f32[1152]{0:T(1024)}, u32[]{:S(2)}) copy-start(f32[1152]{0:T(1024)} %param.28) | copy-start | bytes 13828
  458.2 7.7 %collective-permute-start.6 = (f32[24768]{0:T(1024)}, f32[24768]{0:T(1024)}, u32[]{:S(2)}, u32[]{:S(2)}) collective-permute-start(f32[24768]{0:T(1024)} %concatenate.57), channel_id=1, source_target_pairs={{0,4},{4,0},{8,12},{12,8},{1,5},{5,1},{9,13},{13,9},{2,6},{6,2},{1... | collective-permute-start | bytes 297224 | tf_op jit(solution)/shard_map/ppermute | solution.py:96
  463.4 16.4 %copy-start.3 = (bf16[3,256,1152]{2,1,0:T(8,128)(2,1)S(1)}, bf16[3,256,1152]{2,1,0:T(8,128)(2,1)}, u32[]{:S(2)}) copy-start(bf16[3,256,1152]{2,1,0:T(8,128)(2,1)} %param.17) | copy-start | bytes 5308420
  463.4 16.4 %copy-start.9 = (bf16[3,256,1152]{2,1,0:T(8,128)(2,1)S(1)}, bf16[3,256,1152]{2,1,0:T(8,128)(2,1)}, u32[]{:S(2)}) copy-start(bf16[3,256,1152]{2,1,0:T(8,128)(2,1)} %get-tuple-element.176) | copy-start | bytes 5308420
  466.9 11.4 %collective-permute-start.7 = (f32[24768]{0:T(1024)S(1)}, f32[24768]{0:T(1024)S(1)}, u32[]{:S(2)}, u32[]{:S(2)}) collective-permute-start(f32[24768]{0:T(1024)S(1)} %add.234), channel_id=1, source_target_pairs={{0,8},{4,12},{8,0},{12,4},{1,9},{5,13},{9,1},{13,5},{2,10},{6,14},... | collective-permute-start | bytes 297224 | tf_op jit(solution)/shard_map/ppermute | solution.py:96
  478.2 5.6 collective-permute-start.8
  486.5 6.9 %copy-start.49 = (bf16[3,1152]{1,0:T(4,128)(2,1)S(1)}, bf16[3,1152]{1,0:T(4,128)(2,1)}, u32[]{:S(2)}) copy-start(bf16[3,1152]{1,0:T(4,128)(2,1)} %copy-done.48) | copy-start | bytes 20740
  486.5 6.9 %copy-start.51 = (bf16[3,1152]{1,0:T(4,128)(2,1)S(1)}, bf16[3,1152]{1,0:T(4,128)(2,1)}, u32[]{:S(2)}) copy-start(bf16[3,1152]{1,0:T(4,128)(2,1)} %copy-done.50) | copy-start | bytes 20740
  492.0 10.3 %collective-permute-start.9 = (f32[3,576]{1,0:T(4,128)S(1)}, f32[3,576]{1,0:T(4,128)S(1)}, u32[]{:S(2)}, u32[]{:S(2)}) collective-permute-start(f32[3,576]{1,0:T(4,128)S(1)} %slice_select_fusion.3), channel_id=1, source_target_pairs={{0,16},{16,0},{1,17},{17,1},{2,18},{18,2},{3,19},{19,3},{4,20},{20... | collective-permute-start | bytes 20744 | tf_op jit(solution)/shard_map/ppermute | solution.py:96
  493.3 8.9 %copy-start.53 = (bf16[3,1152]{1,0:T(4,128)(2,1)S(1)}, bf16[3,1152]{1,0:T(4,128)(2,1)}, u32[]{:S(2)}) copy-start(bf16[3,1152]{1,0:T(4,128)(2,1)} %param.18) | copy-start | bytes 20740
  (49 other events, 131.8 us)
Sparse Core Ops, SparseCore 0:
  123.6 44.2 all-reduce.6
  192.4 46.0 all-reduce.8
  372.3 73.3 all-reduce.10
  466.0 154.0 all-reduce.12
where the time goes:
time: 644 us; the launch traced here: 635 us
  waiting for transfers between devices  345 us (54%)
  other arithmetic  86.8 us (13%)
  matrix products  85 us (13%)
  local copies, waits for them, and re-layouts  66.3 us (10%)
  starting transfers between devices  36.9 us (6%)
  between operations  15.1 us (2%)
    psum x1, waiting for transfers between devices, local(): lax.psum(scatter_shard(grad_qkv_weight, 0).astype(jnp.bfloat16), 'ctx')  117 us
    psum x1, waiting for transfers between devices, local(): lax.psum(jnp.dot(activated, down_full, preferred_element_type=jnp.float32...  56.7 us
    psum x1, waiting for transfers between devices, local(): lax.psum(jnp.dot(attn_rows, out_full, preferred_element_type=jnp.float32)...  38 us
    psum x1, waiting for transfers between devices, local(): lax.psum(contract_cols(grad_up_low, up_full).astype(jnp.bfloat16), 'tp')  35.9 us
    ppermute x14, waiting for transfers between devices, swap(): return lax.ppermute(values, axis, [(i, i ^ distance) for i in range(count)])  28.3 us
    all_to_all x1, waiting for transfers between devices, local(): lax.all_to_all(grad_packed_heads, 'ctx', split_axis=1, concat_axis=2, til...  28.2 us
    all_to_all x1, waiting for transfers between devices, local(): lax.all_to_all(packed, 'ctx', split_axis=2, concat_axis=1, tiled=True)  25.8 us
    dot_general x5, matrix products, contract_rows(): lax.dot_general(left, right, (((0,), (0,)), ((), ())), preferred_element_...  24.4 us
  transfers between devices with their start and end apart: 22, of which 11 were waited for; matrix products, arithmetic and copies ran while one was open for 29% of the time, Pallas kernels for 0%

commit v1 on v0

--- a/solution.py
+++ b/solution.py
@@ -255,7 +255,12 @@
     )
     grad_heads = lax.all_to_all(grad_attended, "ctx", split_axis=2, concat_axis=1, tiled=True)
     grad_packed_heads = lax.map(attend_backward, (head_packed, log_total, grad_heads))
-    grad_packed = lax.all_to_all(grad_packed_heads, "ctx", split_axis=1, concat_axis=2, tiled=True)
+    grad_packed = jnp.concatenate(
+        lax.all_to_all(
+            jnp.stack(jnp.split(grad_packed_heads, lax.axis_size("ctx"), axis=1)), "ctx", 0, 0
+        ),
+        axis=2,
+    )
     bias_sums = jnp.sum(grad_packed.astype(jnp.float32), (0, 1))
     grad_qv_bias = jnp.concatenate([bias_sums[:, :head_size], bias_sums[:, 2 * head_size :]], 1)
     grad_packed_rows = grad_packed.reshape(row_count, head_local * 3 * head_size)

time: 644 us -> 622 us (0.966)
  waiting for transfers between devices: 345 us -> 330 us
  local copies, waits for them, and re-layouts: 66.3 us -> 57.4 us
    all_to_all x1, waiting for transfers between devices: 28.2 us -> 11.7 us  [local(): lax.all_to_all(jnp.stack(jnp.split(grad_packed_heads, lax.axis_size('ctx'...]
    all_to_all x2 -> x0, local copies, waits for them, and re-layouts: 8.61 us -> none  [local(): lax.all_to_all(grad_packed_heads, 'ctx', split_axis=1, concat_axis=2, til...]
    another operation x0 -> x3, local copies, waits for them, and re-layouts: none -> 6.44 us  [the longest x1 4.19 us: local(): grad_packed.reshape(row_count, head_local * 3 * head_size)]
    unnamed x151 -> x149, local copies, waits for them, and re-layouts: 16.6 us -> 16.6 us
where the time goes in v1:
time: 622 us; the launch traced here: 613 us
  waiting for transfers between devices  330 us (53%)
  other arithmetic  88.9 us (14%)
  matrix products  84.8 us (14%)
  local copies, waits for them, and re-layouts  57.4 us (9%)
  starting transfers between devices  36.9 us (6%)
  between operations  14.9 us (2%)
    psum x1, waiting for transfers between devices, local(): lax.psum(scatter_shard(grad_qkv_weight, 0).astype(jnp.bfloat16), 'ctx')  117 us
    psum x1, waiting for transfers between devices, local(): lax.psum(jnp.dot(activated, down_full, preferred_element_type=jnp.float32...  58 us
    psum x1, waiting for transfers between devices, local(): lax.psum(jnp.dot(attn_rows, out_full, preferred_element_type=jnp.float32)...  38 us
    psum x1, waiting for transfers between devices, local(): lax.psum(contract_cols(grad_up_low, up_full).astype(jnp.bfloat16), 'tp')  35.9 us
    ppermute x14, waiting for transfers between devices, swap(): return lax.ppermute(values, axis, [(i, i ^ distance) for i in range(count)])  28.3 us
    all_to_all x1, waiting for transfers between devices, local(): lax.all_to_all(packed, 'ctx', split_axis=2, concat_axis=1, tiled=True)  25.8 us
    dot_general x5, matrix products, contract_rows(): lax.dot_general(left, right, (((0,), (0,)), ((), ())), preferred_element_...  24.4 us
    dot_general x5, matrix products, contract_cols(): lax.dot_general(left, right, (((1,), (1,)), ((), ())), preferred_element_...  22.9 us
  transfers between devices with their start and end apart: 22, of which 11 were waited for; matrix products, arithmetic and copies ran while one was open for 29% of the time, Pallas kernels for 0%

profile of v1, /device:TPU:0, one launch (start us, length us, event | category | flops | bytes accessed | tf_op | source)
XLA Modules:
  0.0 613.0 jit_solution(12064170970771255064)
XLA Ops:
  8.1 3.0 collective-permute-start
  16.5 4.4 fusion.83
  23.2 16.3 %collective-permute-done.1 = f32[3,6912]{1,0:T(4,128)S(1)} collective-permute-done((f32[3,6912]{1,0:T(4,128)S(1)}, f32[3,6912]{1,0:T(4,128)S(1)}, u32[]{:S(2)}, u32[]{:S(2)}) %collective-permute-start.1) | collective-permute-done | bytes 82976 | tf_op jit(solution)/shard_map/ppermute | solution.py:96
  40.9 2.5 fusion.40
  48.7 4.0 add_convert_fusion.4
  53.8 4.9 all-to-all-start
  63.5 25.8 %all-to-all-done = bf16[3,256,4,216]{1,3,0,2:T(8,128)(2,1)S(1)} async-done(((bf16[3,256,4,216]{1,3,0,2:T(8,128)(2,1)}), bf16[3,256,4,216]{1,3,0,2:T(8,128)(2,1)S(1)}, u32[]{:S(2)}, u32[]{:S(2)}) %all-to-all-start) | async-done | bytes 1327136 | tf_op jit(solution)/shard_map/all_to_all | solution.py:197
  89.5 9.3 %while.22 = (s32[]{:T(128)}, bf16[3,1024,1,72]{1,3,2,0:T(8,128)(2,1)S(1)}, f32[3,1,1024]{2,1,0:T(1,128)}, bf16[3,1024,1,216]{1,3,2,0:T(8,128)(2,1)S(1)}, s32[]{:T(128)}) while((s32[]{:T(128)}, bf16[3,1024,1,72]{1,3,2,0:T(8,128)(2,1)S(1)}, f32[3,1,1024]{2,1,0:T(1,128)}, bf16[3,1024,1,216]{1,3,2,0:T(8,128)(2,1)S(1)}, s32[]{:T(128)}) %tuple.105), condition=%wide.region_5.6_spmd, body=%wide.region_2.5_spmd.sunk | while | flops 311499776 | bytes 14098513 | solution.py:62
  101.7 3.5 all-to-all-start.1
  107.8 9.5 %all-to-all-done.1 = bf16[4,2,27648]{2,1,0:T(2,128)(2,1)S(1)} async-done(((bf16[4,2,27648]{2,1,0:T(2,128)(2,1)}), bf16[4,2,27648]{2,1,0:T(2,128)(2,1)S(1)}, u32[]{:S(2)}, u32[]{:S(2)}) %all-to-all-start.1) | async-done | bytes 442400 | tf_op jit(solution)/shard_map/all_to_all | solution.py:199
  123.6 3.1 broadcast_select_fusion.3
  126.7 3.2 broadcast_select_fusion.1
  129.9 38.0 %all-reduce.7.cloned.1.call-done = bf16[768,1152]{1,0:T(8,128)(2,1)} async-done(((bf16[768,1152]{1,0:T(8,128)(2,1)}), bf16[768,1152]{1,0:T(8,128)(2,1)}) %all-reduce.7.cloned.1.call-update) | async-done | bytes 1769488 | tf_op jit(solution)/shard_map/psum | solution.py:203
  173.8 2.7 convolution_add_fusion
  176.5 5.0 fusion.86
  181.5 6.7 %fusion.94 = (f32[1152]{0:T(1024)}, bf16[768,1152]{1,0:T(8,128)(2,1)S(1)}) fusion(f32[768,1152]{1,0:T(8,128)S(1)} %convolution_add_fusion, bf16[768,1152]{1,0:T(8,128)(2,1)S(1)} %bitcast.212, bf16[1152,576]{0,1:T(8,128)(2,1)S(1)} %copy-done.28, bf16[1152,576]{0,1:T(8,128)(2,1)S(1)} %copy-done.27), kind=kOutput, calls=%fused_computation.205 | convolution fusion | flops 2065857408 | bytes 9736704 | tf_op jit(solution)/shard_map/dot_general | solution.py:37
  188.2 3.8 convolution_convert_fusion.1
  192.1 4.0 select_convert_fusion
  197.6 4.9 fusion.60
  202.4 35.9 %all-reduce.9.cloned.1.call-done = bf16[3,256,1152]{2,1,0:T(8,128)(2,1)} async-done(((bf16[3,256,1152]{2,1,0:T(8,128)(2,1)}), bf16[3,256,1152]{2,1,0:T(8,128)(2,1)}) %all-reduce.9.cloned.1.call-update) | async-done | bytes 1769488 | tf_op jit(solution)/shard_map/psum | solution.py:239
  243.1 2.9 multiply_reduce_fusion.4
  255.1 5.0 all-to-all-start.2
  260.1 7.2 %convolution_convert_fusion.2 = bf16[768,1152]{1,0:T(8,128)(2,1)} fusion(bf16[1152,576]{0,1:T(8,128)(2,1)} %get-tuple-element.174, bf16[1152,576]{0,1:T(8,128)(2,1)} %get-tuple-element.173, f32[768,1152]{1,0:T(8,128)} %copy-done.69), kind=kOutput, calls=%fused_computation.96 | convolution fusion | flops 2052587520 | bytes 7962624 | tf_op jit(solution)/shard_map/dot_general | solution.py:220
  267.3 5.6 all-to-all-done.2
  274.7 23.1 %while.23 = (s32[]{:T(128)}, bf16[3,1024,1,216]{1,3,2,0:T(8,128)(2,1)}, bf16[3,1024,1,216]{1,3,2,0:T(8,128)(2,1)}, f32[3,1,1024]{2,1,0:T(1,128)}, bf16[3,1024,1,72]{1,3,2,0:T(8,128)(2,1)}, /*index=5*/s32[]{:T(128)}) while((s32[]{:T(128)}, bf16[3,1024,1,216]{1,3,2,0:T(8,128)(2,1)}, bf16[3,1024,1,216]{1,3,2,0:T(8,128)(2,1)}, ...), condition=%wide.region_15.16_spmd, body=%wide.region_13.15_spmd.sunk | while | flops 769252352 | bytes 36499580 | solution.py:257
  301.2 4.3 all-to-all-start.3
  309.6 3.9 select_convert_fusion.1
  315.9 3.8 collective-permute-done.11
  320.7 4.4 add_convert_fusion.2
  325.1 11.7 %all-to-all-done.3 = bf16[4,3,256,1,216]{2,4,1,3,0:T(8,128)(2,1)} async-done(((bf16[4,3,256,1,216]{2,4,1,3,0:T(8,128)(2,1)}), bf16[4,3,256,1,216]{2,4,1,3,0:T(8,128)(2,1)}, u32[]{:S(2)}, u32[]{:S(2)}) %all-to-all-start.3) | async-done | bytes 1327136 | tf_op jit(solution)/shard_map/all_to_all | solution.py:259
  336.8 3.8 copy.151
  340.6 4.2 reshape_reshape.3
  344.7 5.3 convolution_convert_fusion
  350.2 4.4 add_convert_fusion.3
  357.0 3.9 fusion.95
  365.6 58.0 %all-reduce.11.cloned.1.call-done = (bf16[768,1152]{1,0:T(8,128)(2,1)}, bf16[3,256,1152]{2,1,0:T(8,128)(2,1)}) async-done(((bf16[768,1152]{1,0:T(8,128)(2,1)}, bf16[3,256,1152]{2,1,0:T(8,128)(2,1)}), (bf16[768,1152]{1,0:T(8,128)(2,1)}, bf16[3,256,1152]{2,1,0:T(8,128)(2,1)})) %all-reduce.11.cloned.1.call-update) | async-done | bytes 3538960 | tf_op jit(solution)/shard_map/psum | solution.py:219
  423.7 3.0 fusion.46
  426.7 2.7 fusion.51
  430.9 2.8 fusion.33
  437.6 3.7 add_convert_fusion.5
  441.3 2.5 copy.154
  444.8 2.5 collective-permute-start.7
  447.9 8.2 %collective-permute-done.7 = f32[24768]{0:T(1024)S(1)} collective-permute-done((f32[24768]{0:T(1024)S(1)}, f32[24768]{0:T(1024)S(1)}, u32[]{:S(2)}, u32[]{:S(2)}) %collective-permute-start.7) | collective-permute-done | bytes 99104 | tf_op jit(solution)/shard_map/ppermute | solution.py:96
  457.7 4.1 add_add_fusion.2
  464.4 5.5 fusion.64
  471.2 8.2 %fusion.63 = f32[576,6912]{1,0:T(8,128)} fusion(bf16[3,6912]{1,0:T(4,128)(2,1)S(1)} %get-tuple-element.187, bf16[3,6912]{1,0:T(4,128)(2,1)S(1)} %get-tuple-element.185, s32[]{:T(128)S(6)} %select_n.170, bf16[3,1152]{1,0:T(4,128)(2,1)S(1)} %copy-done.50, bf16[3,1152]{1,0:T(4,128)(2,1)S(1)} %copy-done.48), kind=kOutput, calls=%fused_computation.142 | convolution fusion | flops 47955456 | bytes 16022020 | tf_op jit(solution)/shard_map/dot_general | solution.py:31
  480.8 117.2 %all-reduce.13.cloned.1.call-done = (bf16[576,4,216]{0,2,1:T(8,128)(2,1)}, bf16[288,576]{1,0:T(8,128)(2,1)}, bf16[576,1152]{1,0:T(8,128)(2,1)}, bf16[1152,576]{0,1:T(8,128)(2,1)}) async-done(((bf16[576,4,216]{0,2,1:T(8,128)(2,1)}, bf16[288,576]{1,0:T(8,128)(2,1)}, bf16[576,1152]{1,0:T(8,128)(2,1)}, bf16[1152,576]{0,1:T(8,128)(2,1)}), (bf16[576,4,216]{0,2,1:T(8,128)(2,1)}, bf16[288,576]{1,0:T(8,128)(2,1)}, ...) | async-done | bytes 3981328 | tf_op jit(solution)/shard_map/psum | solution.py:337
  600.0 2.8 reshape.375
  (316 shorter events, 125.4 us)
Async XLA Ops:
  7.2 8.7 %copy-start.51 = (bf16[3,1152]{1,0:T(4,128)(2,1)S(1)}, bf16[3,1152]{1,0:T(4,128)(2,1)}, u32[]{:S(2)}) copy-start(bf16[3,1152]{1,0:T(4,128)(2,1)} %param.18) | copy-start | bytes 20740
  7.2 7.5 %copy-start = (bf16[3,256,1152]{2,1,0:T(8,128)(2,1)S(1)}, bf16[3,256,1152]{2,1,0:T(8,128)(2,1)}, u32[]{:S(2)}) copy-start(bf16[3,256,1152]{2,1,0:T(8,128)(2,1)} %param.17) | copy-start | bytes 5308420
  7.2 8.1 %copy-start.67 = (f32[4,144]{1,0:T(4,128)S(1)}, f32[4,144]{1,0:T(4,128)}, u32[]{:S(2)}) copy-start(f32[4,144]{1,0:T(4,128)} %param.22) | copy-start | bytes 6916
  8.1 7.8 %collective-permute-start = (bf16[3,1152]{1,0:T(4,128)(2,1)S(1)}, bf16[3,1152]{1,0:T(4,128)(2,1)S(1)}, u32[]{:S(2)}, u32[]{:S(2)}) collective-permute-start(bf16[3,1152]{1,0:T(4,128)(2,1)S(1)} %fusion.68), channel_id=1, source_target_pairs={{0,16},{16,0},{1,17},{17,1},{2,18},{18,2},{3,19},{19,3},{4,20},{20... | collective-permute-start | bytes 20744 | tf_op jit(solution)/shard_map/ppermute | solution.py:96
  12.8 30.6 %collective-permute-start.2 = (bf16[576,864]{1,0:T(8,128)(2,1)S(1)}, bf16[576,864]{1,0:T(8,128)(2,1)}, u32[]{:S(2)}, u32[]{:S(2)}) collective-permute-start(bf16[576,864]{1,0:T(8,128)(2,1)S(1)} %copy.135), channel_id=1, source_target_pairs={{0,16},{16,0},{1,17},{17,1},{2,18},{18,2},{3,19},{19,3},{4,20},{20... | collective-permute-start | bytes 2985992 | tf_op jit(solution)/shard_map/ppermute | solution.py:96
  14.7 26.2 %copy-start.44 = (f32[3,256]{1,0:T(4,128)}, f32[3,256]{1,0:T(4,128)S(1)}, u32[]{:S(2)}) copy-start(f32[3,256]{1,0:T(4,128)S(1)} %broadcast_multiply_fusion.1) | copy-start | bytes 9220
  15.3 25.6 %copy-start.57 = (f32[3,256]{1,0:T(4,128)}, f32[3,256]{1,0:T(4,128)S(1)}, u32[]{:S(2)}) copy-start(f32[3,256]{1,0:T(4,128)S(1)} %fusion.72) | copy-start | bytes 9220
  16.5 22.9 %copy-start.63 = (f32[6912]{0:T(1024)S(1)}, f32[6912]{0:T(1024)}, u32[]{:S(2)}) copy-start(f32[6912]{0:T(1024)} %param.20) | copy-start | bytes 82948
  21.0 18.4 %collective-permute-start.1 = (f32[3,6912]{1,0:T(4,128)S(1)}, f32[3,6912]{1,0:T(4,128)S(1)}, u32[]{:S(2)}, u32[]{:S(2)}) collective-permute-start(f32[3,6912]{1,0:T(4,128)S(1)} %slice_select_fusion), channel_id=1, source_target_pairs={{0,16},{16,0},{1,17},{17,1},{2,18},{18,2},{3,19},{19,3},{4,20},{20... | collective-permute-start | bytes 248840 | tf_op jit(solution)/shard_map/ppermute | solution.py:96
  52.7 8.6 %copy-start.11 = (bf16[3,256,1152]{2,1,0:T(8,128)(2,1)S(1)}, bf16[3,256,1152]{2,1,0:T(8,128)(2,1)}, u32[]{:S(2)}) copy-start(bf16[3,256,1152]{2,1,0:T(8,128)(2,1)} %param.29) | copy-start | bytes 5308420
  53.8 35.5 %all-to-all-start = ((bf16[3,256,4,216]{1,3,0,2:T(8,128)(2,1)}), bf16[3,256,4,216]{1,3,0,2:T(8,128)(2,1)S(1)}, u32[]{:S(2)}, u32[]{:S(2)}) async-start(bf16[3,256,4,216]{1,3,0,2:T(8,128)(2,1)} %copy.138), calls=%async_computation | async-start | bytes 2654208 | tf_op jit(solution)/shard_map/all_to_all | solution.py:197
  58.7 47.9 %collective-permute-start.3 = (bf16[288,576]{1,0:T(8,128)(2,1)}, bf16[288,576]{1,0:T(8,128)(2,1)}, u32[]{:S(2)}, u32[]{:S(2)}) collective-permute-start(bf16[288,576]{1,0:T(8,128)(2,1)} %param.23), channel_id=1, source_target_pairs={{0,16},{16,0},{1,17},{17,1},{2,18},{18,2},{3,19},{19,3},{4,20},{20... | collective-permute-start | bytes 995336 | tf_op jit(solution)/shard_map/ppermute | solution.py:96
  59.2 64.3 %collective-permute-start.4 = (bf16[576,1152]{1,0:T(8,128)(2,1)}, bf16[576,1152]{1,0:T(8,128)(2,1)}, u32[]{:S(2)}, u32[]{:S(2)}) collective-permute-start(bf16[576,1152]{1,0:T(8,128)(2,1)} %param.25), channel_id=1, source_target_pairs={{0,16},{16,0},{1,17},{17,1},{2,18},{18,2},{3,19},{19,3},{4,20},{20... | collective-permute-start | bytes 3981320 | tf_op jit(solution)/shard_map/ppermute | solution.py:96
  60.7 66.0 %collective-permute-start.5 = (bf16[1152,576]{0,1:T(8,128)(2,1)}, bf16[1152,576]{0,1:T(8,128)(2,1)}, u32[]{:S(2)}, u32[]{:S(2)}) collective-permute-start(bf16[1152,576]{0,1:T(8,128)(2,1)} %param.27), channel_id=1, source_target_pairs={{0,16},{16,0},{1,17},{17,1},{2,18},{18,2},{3,19},{19,3},{4,20},{20... | collective-permute-start | bytes 3981320 | tf_op jit(solution)/shard_map/ppermute | solution.py:96
  98.8 21.0 %copy-start.7 = (bf16[3,1024,1,216]{1,3,2,0:T(8,128)(2,1)}, bf16[3,1024,1,216]{1,3,2,0:T(8,128)(2,1)S(1)}, u32[]{:S(2)}) copy-start(bf16[3,1024,1,216]{1,3,2,0:T(8,128)(2,1)S(1)} %get-tuple-element.325) | copy-start | bytes 3981316
  98.8 6.6 %copy-start.59 = (f32[3,1,1152]{2,1,0:T(1,128)S(1)}, f32[3,1,1152]{2,1,0:T(1,128)}, u32[]{:S(2)}) copy-start(f32[3,1,1152]{2,1,0:T(1,128)} %get-tuple-element.189) | copy-start | bytes 41476
  98.8 6.6 %copy-start.60 = (f32[3,1,1152]{2,1,0:T(1,128)S(1)}, f32[3,1,1152]{2,1,0:T(1,128)}, u32[]{:S(2)}) copy-start(f32[3,1,1152]{2,1,0:T(1,128)} %get-tuple-element.190) | copy-start | bytes 41476
  101.7 15.7 %all-to-all-start.1 = ((bf16[4,2,27648]{2,1,0:T(2,128)(2,1)}), bf16[4,2,27648]{2,1,0:T(2,128)(2,1)S(1)}, u32[]{:S(2)}, u32[]{:S(2)}) async-start(bf16[4,2,27648]{2,1,0:T(2,128)(2,1)} %reshape.412), calls=%async_computation.1 | async-start | bytes 884736 | tf_op jit(solution)/shard_map/all_to_all | solution.py:199
  105.2 62.7 %all-reduce.7.cloned.1.call-start = ((), (), s32[]{:S(2)}) async-start(), calls=%async_computation.4 | async-start | bytes 3538944 | tf_op jit(solution)/shard_map/psum | solution.py:203
  107.8 15.6 %copy-start.37 = (bf16[288,576]{1,0:T(8,128)(2,1)}, bf16[288,576]{1,0:T(8,128)(2,1)S(1)}, u32[]{:S(2)}) copy-start(bf16[288,576]{1,0:T(8,128)(2,1)S(1)} %get-tuple-element.180) | copy-start | bytes 995332
  107.8 15.6 %copy-start.39 = (bf16[288,576]{1,0:T(8,128)(2,1)}, bf16[288,576]{1,0:T(8,128)(2,1)S(1)}, u32[]{:S(2)}) copy-start(bf16[288,576]{1,0:T(8,128)(2,1)S(1)} %get-tuple-element.181) | copy-start | bytes 995332
  123.5 114.8 %all-reduce.9.cloned.1.call-start = ((), (), s32[]{:S(2)}) async-start(), calls=%async_computation.5 | async-start | bytes 3538944 | tf_op jit(solution)/shard_map/psum | solution.py:239
  126.7 41.2 %copy-start.65 = (f32[1152]{0:T(1024)S(1)}, f32[1152]{0:T(1024)}, u32[]{:S(2)}) copy-start(f32[1152]{0:T(1024)} %param.24) | copy-start | bytes 13828
  196.1 124.6 %collective-permute-start.13 = (bf16[1152,576]{0,1:T(8,128)(2,1)}, bf16[1152,576]{0,1:T(8,128)(2,1)}, u32[]{:S(2)}, u32[]{:S(2)}) collective-permute-start(bf16[1152,576]{0,1:T(8,128)(2,1)} %select_convert_fusion), channel_id=1, source_target_pairs={{0,16},{16,0},{1,17},{17,1},{2,18},{18,2},{3,19},{19,3},{4,20},{20... | collective-permute-start | bytes 3981320 | tf_op jit(solution)/shard_map/ppermute | solution.py:96
  255.1 17.8 %all-to-all-start.2 = ((bf16[3,256,4,72]{1,3,0,2:T(8,128)(2,1)}), bf16[3,256,4,72]{1,3,0,2:T(8,128)(2,1)}, u32[]{:S(2)}, u32[]{:S(2)}) async-start(bf16[3,256,4,72]{1,3,0,2:T(8,128)(2,1)} %copy.144), calls=%async_computation.2 | async-start | bytes 884736 | tf_op jit(solution)/shard_map/all_to_all | solution.py:256
  301.2 35.6 %all-to-all-start.3 = ((bf16[4,3,256,1,216]{2,4,1,3,0:T(8,128)(2,1)}), bf16[4,3,256,1,216]{2,4,1,3,0:T(8,128)(2,1)}, u32[]{:S(2)}, u32[]{:S(2)}) async-start(bf16[4,3,256,1,216]{2,4,1,3,0:T(8,128)(2,1)} %pad_maximum_fusion.10), calls=%async_computation.3 | async-start | bytes 2654208 | tf_op jit(solution)/shard_map/all_to_all | solution.py:259
  305.5 118.1 %all-reduce.11.cloned.1.call-start = ((), (), s32[]{:S(2)}) async-start(), calls=%async_computation.6 | async-start | bytes 7077888 | tf_op jit(solution)/shard_map/psum | solution.py:219
  307.9 6.2 %copy-start.54 = (f32[3,1152]{1,0:T(4,128)S(1)}, f32[3,1152]{1,0:T(4,128)}, u32[]{:S(2)}) copy-start(f32[3,1152]{1,0:T(4,128)} %get-tuple-element.129) | copy-start | bytes 41476
  307.9 6.8 %copy-start.55 = (f32[3,1152]{1,0:T(4,128)S(1)}, f32[3,1152]{1,0:T(4,128)}, u32[]{:S(2)}) copy-start(f32[3,1152]{1,0:T(4,128)} %get-tuple-element.134) | copy-start | bytes 41476
  307.9 7.4 %copy-start.53 = (f32[3,1152]{1,0:T(4,128)S(1)}, f32[3,1152]{1,0:T(4,128)}, u32[]{:S(2)}) copy-start(f32[3,1152]{1,0:T(4,128)} %get-tuple-element.137) | copy-start | bytes 41476
  308.1 11.6 %collective-permute-start.11 = (bf16[288,576]{1,0:T(8,128)(2,1)S(1)}, bf16[288,576]{1,0:T(8,128)(2,1)S(1)}, u32[]{:S(2)}, u32[]{:S(2)}) collective-permute-start(bf16[288,576]{1,0:T(8,128)(2,1)S(1)} %select_convert_fusion.3), channel_id=1, source_target_pairs={{0,16},{16,0},{1,17},{17,1},{2,18},{18,2},{3,19},{19,3},{4,20},{20... | collective-permute-start | bytes 995336 | tf_op jit(solution)/shard_map/ppermute | solution.py:96
  313.5 36.7 %collective-permute-start.12 = (bf16[576,1152]{1,0:T(8,128)(2,1)}, bf16[576,1152]{1,0:T(8,128)(2,1)}, u32[]{:S(2)}, u32[]{:S(2)}) collective-permute-start(bf16[576,1152]{1,0:T(8,128)(2,1)} %select_convert_fusion.1), channel_id=1, source_target_pairs={{0,16},{16,0},{1,17},{17,1},{2,18},{18,2},{3,19},{19,3},{4,20},{20... | collective-permute-start | bytes 3981320 | tf_op jit(solution)/shard_map/ppermute | solution.py:96
  350.1 247.9 %all-reduce.13.cloned.1.call-start = ((), (), s32[]{:S(2)}) async-start(), calls=%async_computation.7 | async-start | bytes 8257536 | tf_op jit(solution)/shard_map/psum | solution.py:337
  357.0 66.6 %copy-start.45 = (f32[3,256]{1,0:T(4,128)S(1)}, f32[3,256]{1,0:T(4,128)}, u32[]{:S(2)}) copy-start(f32[3,256]{1,0:T(4,128)} %copy-done.44) | copy-start | bytes 9220
  362.9 63.7 %copy-start.62 = (f32[3,256]{1,0:T(4,128)S(1)}, f32[3,256]{1,0:T(4,128)}, u32[]{:S(2)}) copy-start(f32[3,256]{1,0:T(4,128)} %copy-done.61) | copy-start | bytes 9220
  362.9 63.7 %copy-start.58 = (f32[3,256]{1,0:T(4,128)S(1)}, f32[3,256]{1,0:T(4,128)}, u32[]{:S(2)}) copy-start(f32[3,256]{1,0:T(4,128)} %copy-done.57) | copy-start | bytes 9220
  364.1 73.5 %collective-permute-start.10 = (bf16[576,864]{1,0:T(8,128)(2,1)}, bf16[576,864]{1,0:T(8,128)(2,1)}, u32[]{:S(2)}, u32[]{:S(2)}) collective-permute-start(bf16[576,864]{1,0:T(8,128)(2,1)} %select_convert_fusion.2), channel_id=1, source_target_pairs={{0,16},{16,0},{1,17},{17,1},{2,18},{18,2},{3,19},{19,3},{4,20},{20... | collective-permute-start | bytes 2985992 | tf_op jit(solution)/shard_map/ppermute | solution.py:96
  423.6 7.0 %copy-start.22 = (bf16[768,1152]{1,0:T(8,128)(2,1)S(1)}, bf16[768,1152]{1,0:T(8,128)(2,1)}, u32[]{:S(2)}) copy-start(bf16[768,1152]{1,0:T(8,128)(2,1)} %get-tuple-element.157) | copy-start | bytes 5308420
  423.6 7.0 %copy-start.66 = (f32[1152]{0:T(1024)S(1)}, f32[1152]{0:T(1024)}, u32[]{:S(2)}) copy-start(f32[1152]{0:T(1024)} %param.28) | copy-start | bytes 13828
  436.1 7.7 %collective-permute-start.6 = (f32[24768]{0:T(1024)}, f32[24768]{0:T(1024)}, u32[]{:S(2)}, u32[]{:S(2)}) collective-permute-start(f32[24768]{0:T(1024)} %concatenate.57), channel_id=1, source_target_pairs={{0,4},{4,0},{8,12},{12,8},{1,5},{5,1},{9,13},{13,9},{2,6},{6,2},{1... | collective-permute-start | bytes 297224 | tf_op jit(solution)/shard_map/ppermute | solution.py:96
  441.3 16.4 %copy-start.3 = (bf16[3,256,1152]{2,1,0:T(8,128)(2,1)S(1)}, bf16[3,256,1152]{2,1,0:T(8,128)(2,1)}, u32[]{:S(2)}) copy-start(bf16[3,256,1152]{2,1,0:T(8,128)(2,1)} %param.17) | copy-start | bytes 5308420
  441.3 16.4 %copy-start.9 = (bf16[3,256,1152]{2,1,0:T(8,128)(2,1)S(1)}, bf16[3,256,1152]{2,1,0:T(8,128)(2,1)}, u32[]{:S(2)}) copy-start(bf16[3,256,1152]{2,1,0:T(8,128)(2,1)} %get-tuple-element.158) | copy-start | bytes 5308420
  444.8 11.3 %collective-permute-start.7 = (f32[24768]{0:T(1024)S(1)}, f32[24768]{0:T(1024)S(1)}, u32[]{:S(2)}, u32[]{:S(2)}) collective-permute-start(f32[24768]{0:T(1024)S(1)} %add.234), channel_id=1, source_target_pairs={{0,8},{4,12},{8,0},{12,4},{1,9},{5,13},{9,1},{13,5},{2,10},{6,14},... | collective-permute-start | bytes 297224 | tf_op jit(solution)/shard_map/ppermute | solution.py:96
  456.2 5.6 collective-permute-start.8
  464.4 6.9 %copy-start.48 = (bf16[3,1152]{1,0:T(4,128)(2,1)S(1)}, bf16[3,1152]{1,0:T(4,128)(2,1)}, u32[]{:S(2)}) copy-start(bf16[3,1152]{1,0:T(4,128)(2,1)} %copy-done.47) | copy-start | bytes 20740
  464.4 6.9 %copy-start.50 = (bf16[3,1152]{1,0:T(4,128)(2,1)S(1)}, bf16[3,1152]{1,0:T(4,128)(2,1)}, u32[]{:S(2)}) copy-start(bf16[3,1152]{1,0:T(4,128)(2,1)} %copy-done.49) | copy-start | bytes 20740
  469.9 10.3 %collective-permute-start.9 = (f32[3,576]{1,0:T(4,128)S(1)}, f32[3,576]{1,0:T(4,128)S(1)}, u32[]{:S(2)}, u32[]{:S(2)}) collective-permute-start(f32[3,576]{1,0:T(4,128)S(1)} %slice_select_fusion.3), channel_id=1, source_target_pairs={{0,16},{16,0},{1,17},{17,1},{2,18},{18,2},{3,19},{19,3},{4,20},{20... | collective-permute-start | bytes 20744 | tf_op jit(solution)/shard_map/ppermute | solution.py:96
  471.2 8.9 %copy-start.52 = (bf16[3,1152]{1,0:T(4,128)(2,1)S(1)}, bf16[3,1152]{1,0:T(4,128)(2,1)}, u32[]{:S(2)}) copy-start(bf16[3,1152]{1,0:T(4,128)(2,1)} %param.18) | copy-start | bytes 20740
  (48 other events, 127.4 us)
Sparse Core Ops, SparseCore 0:
  123.6 44.2 all-reduce.6
  192.2 46.0 all-reduce.8
  350.2 73.3 all-reduce.10
  443.9 154.0 all-reduce.12
